TPU v7x, 256 devices: a whole 4x4x8 slice. The times are simulated.
256 devices in a mesh: outer: 8 (over y, core), inner: 32 (over z, x).
Axes of the slice: x: 4, y: 4, z: 8, core: 2. Of those that a mesh axis runs over, the one named last changes fastest.
Arguments:
- tokens: bfloat16 [98304, 4096], P(('outer', 'inner')), may hold values from -6 to 6
- out_grad: bfloat16 [98304, 1024], P(('outer', 'inner')), may hold values from -0.25 to 0.25
- master_weights: float32 [1024, 4096], P(('outer', 'inner')), may hold values from -0.0421 to 0.0421
- base_weights: bfloat16 [1024, 4096], replicated, may hold values from -0.030029297 to 0.030029297
- adam_m: float32 [1024, 4096], P(('outer', 'inner')), may hold values from -8 to 8
- adam_v: float32 [1024, 4096], P(('outer', 'inner')), may hold values from 0.1 to 10
- grad_exps: int32 [256, 8, 32], P(('outer', 'inner')), may hold values from -13 to -8
- diff_exps: int32 [1024, 32], P(('outer', 'inner')), may hold values from -20 to -15
- hadamard_signs: int32 [32, 128], replicated, may hold values 0 or 1
Outputs:
- projected: bfloat16 [98304, 1024], P(('outer', 'inner'))
- new_master: float32 [1024, 4096], P(('outer', 'inner'))
- new_first: float32 [1024, 4096], P(('outer', 'inner'))
- new_second: float32 [1024, 4096], P(('outer', 'inner'))
All inputs are finite; a program needn't handle non-finite values.
Results may differ from a plain program's by a relative error of at most 0.005.
Values may be sent and summed in bfloat16 or wider, within the bound.
No kernel may reach another device: no remote copies, remote signals or barrier semaphores. Data moves between devices by JAX's collectives and lax.ppermute only.
A program may use at most 128 MiB of HBM per device.

v0:
```python
import math
import jax
import jax.numpy as jnp
from jax import lax
from jax.sharding import Mesh
from jax.sharding import PartitionSpec as P

ADAM_STEP = 10
INNER = ("inner_0", "inner_1")
OUTER_INNER = ("outer", "inner_0", "inner_1")
clip_level = 448.0
beta_one = 0.9
beta_two = 0.95
learn_rate = 0.002
decay_rate = 0.1
adam_eps = 1e-08
highest = lax.Precision.HIGHEST


def summed_rows(terms, axes):
    running = terms.astype(jnp.bfloat16)
    for axis in axes:
        running = lax.psum_scatter(running, axis, scatter_dimension=0, tiled=True)
    return running.astype(jnp.float32)


def in_blocks(value, dim, count):
    before, after = (value.shape[:dim], value.shape[dim + 1 :])
    return jnp.moveaxis(value.reshape(*before, count, -1, *after), dim, 0)


def sum_at_owner(value, axis, dim):
    count = lax.axis_size(axis)
    blocks = lax.all_to_all(in_blocks(value, dim, count), axis, 0, 0, tiled=True)
    return jnp.sum(blocks.astype(jnp.float32), axis=0)


def sent_to_all(value, axis):
    count = lax.axis_size(axis)
    return lax.all_to_all(
        jnp.broadcast_to(value[None], (count, *value.shape)), axis, 0, 0, tiled=True
    )


def joined_along(blocks, dim):
    blocks = jnp.moveaxis(blocks, 0, dim)
    dims = blocks.shape
    return blocks.reshape(*dims[:dim], dims[dim] * dims[dim + 1], *dims[dim + 2 :])


def gathered_copies(value, axis, dim):
    blocks = sent_to_all(value, axis)
    return joined_along(blocks, dim)


def hadamard(matrix_size):
    positions = jnp.arange(matrix_size, dtype=jnp.int32)
    common = positions[:, None] & positions[None, :]
    parity = jnp.zeros((matrix_size, matrix_size), jnp.int32)
    for bit_level in range(matrix_size.bit_length() - 1):
        parity = parity + (common >> bit_level & 1)
    return (1 - 2 * (parity % 2)).astype(jnp.float32)


def rotate_rows(row_block, sign_rows, matrix):
    row_count = row_block.shape[0]
    blocks = row_block.reshape(row_count, sign_rows.shape[0], sign_rows.shape[1]) * sign_rows
    turned = jnp.dot(blocks.reshape(-1, sign_rows.shape[1]), matrix, precision=highest)
    return turned.reshape(row_block.shape) / math.sqrt(sign_rows.shape[1])


def unrotate_rows(row_block, sign_rows, matrix):
    row_count = row_block.shape[0]
    turned = jnp.dot(
        row_block.reshape(-1, sign_rows.shape[1]), matrix, precision=highest
    ) / math.sqrt(sign_rows.shape[1])
    return (turned.reshape(row_count, sign_rows.shape[0], sign_rows.shape[1]) * sign_rows).reshape(
        row_block.shape
    )


def clip_rows(row_block, bound_rows):
    row_count = row_block.shape[0]
    shaped = row_block.reshape(row_count, bound_rows.shape[1], -1)
    limits = bound_rows[:, :, None]
    return jnp.clip(shaped, -limits, limits).reshape(row_block.shape)


def adam_update(gradient, master, first, second):
    new_first = beta_one * first + (1.0 - beta_one) * gradient
    new_second = beta_two * second + (1.0 - beta_two) * gradient * gradient
    fix_one = 1.0 - beta_one**ADAM_STEP
    fix_two = 1.0 - beta_two**ADAM_STEP
    step_dir = new_first / fix_one / (jnp.sqrt(new_second / fix_two) + adam_eps)
    new_master = master - learn_rate * (step_dir + decay_rate * master)
    return (new_master, new_first, new_second)


def shards(
    tokens,
    out_grad,
    master_weights,
    base_weights,
    adam_m,
    adam_v,
    grad_exps,
    diff_exps,
    hadamard_signs,
):
    outer_count = lax.axis_size("outer")
    inner_count = lax.axis_size(INNER)
    token_rows = tokens.shape[0]
    model_width = tokens.shape[1]
    rows_dev = master_weights.shape[0]
    sign_rows = (2 * hadamard_signs - 1).astype(jnp.float32)
    block_len = sign_rows.shape[1]
    col_blocks = sign_rows.shape[0]
    matrix = hadamard(block_len)
    bound_all = jnp.repeat(
        clip_level * jnp.exp2(grad_exps[0].astype(jnp.float32)), block_len, axis=0
    )
    grad_grid = out_grad.reshape(token_rows, outer_count, inner_count, rows_dev).transpose(
        0, 2, 1, 3
    )
    bound_grid = bound_all.reshape(outer_count, inner_count, rows_dev, col_blocks).transpose(
        1, 0, 2, 3
    )
    coded_bound_sel = bound_grid.reshape(-1, col_blocks)
    term_rows = lax.dot_general(
        grad_grid.reshape(token_rows, -1),
        tokens,
        (((0,), (0,)), ((), ())),
        preferred_element_type=jnp.float32,
    )
    turned = rotate_rows(term_rows, sign_rows, matrix)
    coded_rows = lax.optimization_barrier(clip_rows(turned, coded_bound_sel).astype(jnp.bfloat16))
    coded_rows = coded_rows.astype(jnp.float32)
    group_sum = summed_rows(
        coded_rows.reshape(1 * lax.axis_size(INNER), outer_count, rows_dev, model_width), INNER
    )
    summed = sum_at_owner(group_sum.astype(jnp.bfloat16), "outer", 1).reshape(rows_dev, model_width)
    gradient = unrotate_rows(summed, sign_rows, matrix)
    new_master, new_first, new_second = adam_update(gradient, master_weights, adam_m, adam_v)
    owner = lax.axis_index("outer") * inner_count + lax.axis_index(INNER)
    base_own = lax.dynamic_slice_in_dim(base_weights, owner * rows_dev, rows_dev, 0).astype(
        jnp.float32
    )
    diff_bound = clip_level * jnp.exp2(diff_exps.astype(jnp.float32))
    diff_coded = clip_rows(new_master - base_own, diff_bound).astype(jnp.bfloat16)
    outer_part = gathered_copies(diff_coded.reshape(1, 1, rows_dev, model_width), "outer", 0)
    base_grid = base_weights.reshape(outer_count, inner_count, rows_dev, model_width)
    effective = (
        base_grid.astype(jnp.float32)
        + lax.all_gather(outer_part, INNER, axis=1, tiled=True).astype(jnp.float32)
    ).astype(jnp.bfloat16)
    result = lax.dot_general(
        tokens, effective, (((1,), (3,)), ((), ())), preferred_element_type=jnp.float32
    )
    projected = (
        result.reshape(token_rows, outer_count, -1).astype(jnp.bfloat16).reshape(token_rows, -1)
    )
    return (projected, new_master, new_first, new_second)


def solution(mesh):
    split = Mesh(mesh.devices.reshape(mesh.shape["outer"], 8, 4), ("outer", "inner_0", "inner_1"))
    return jax.shard_map(
        shards,
        mesh=split,
        in_specs=(
            P(OUTER_INNER, None),
            P(OUTER_INNER, None),
            P(OUTER_INNER, None),
            P(),
            P(OUTER_INNER, None),
            P(OUTER_INNER, None),
            P(OUTER_INNER, None, None),
            P(OUTER_INNER, None),
            P(),
        ),
        out_specs=(
            P(OUTER_INNER, None),
            P(OUTER_INNER, None),
            P(OUTER_INNER, None),
            P(OUTER_INNER, None),
        ),
        check_vma=False,
    )
```

profile of v0, /device:TPU:1, one launch (start us, length us, event | category | flops | bytes accessed | tf_op | source)
XLA Modules:
  0.0 408.4 jit_solution(3144663483152369432)
XLA Ops:
  7.2 0.0 reduce-scatter.3.cloned.1.call-start
  7.2 0.7 fusion.40
  7.9 3.4 copy.50
  11.4 2.3 copy.38
  13.7 2.4 reshape.73
  16.0 2.3 copy.39
  18.3 2.3 reshape.81
  20.6 5.7 %convolution_multiply_fusion.1 = f32[1024,32,128]{2,0,1:T(8,128)S(1)} fusion(bf16[384,1024,1]{0,1,2:T(8,128)(2,1)} %reshape.81, bf16[32,128,384]{2,1,0:T(8,128)(2,1)S(1)} %bitcast.61, f32[32,128]{1,0:T(8,128)S(1)} %get-tuple-element.25), kind=kOutput, calls=%fused_computation.6 | convolution fusion | flops 3225419776 | bytes 20725760 | tf_op jit(solution)/shard_map/dot_general | solution.py:129
  26.3 20.2 %copy.41 = f32[1024,32,128]{2,1,0:T(8,128)S(1)} copy(f32[1024,32,128]{2,0,1:T(8,128)S(1)} %convolution_multiply_fusion.1) | data formatting | bytes 33554432 | tf_op jit(solution)/shard_map/mul | solution.py:67
  46.4 15.3 %convolution_multiply_fusion = bf16[32768,128]{1,0:T(8,128)(2,1)} fusion(f32[32768,128]{1,0:T(8,128)S(1)} %bitcast.56), kind=kOutput, calls=%fused_computation | convolution fusion | flops 6451412992 | bytes 25165824 | tf_op jit(solution)/shard_map/dot_general | solution.py:68
  61.8 13.4 %div.31 = bf16[1024,4096]{1,0:T(8,128)(2,1)} reshape(bf16[32768,128]{1,0:T(8,128)(2,1)} %convolution_multiply_fusion) | data formatting | bytes 16777216 | tf_op jit(solution)/shard_map/div | solution.py:69
  75.2 0.1 transpose.19
  75.3 0.0 slice-start
  75.3 11.7 %max.32 = bf16[1024,32,128]{2,1,0:T(8,128)(2,1)S(1)} broadcast(bf16[1024,32]{1,0:T(8,128)(2,1)S(1)} %neg.13), dimensions={0,1} | broadcast | bytes 8454144 | tf_op jit(solution)/shard_map/jit(clip)/max | solution.py:86
  87.1 0.0 slice-start.1
  87.1 10.2 %min.35 = bf16[1024,32,128]{2,1,0:T(8,128)(2,1)S(1)} broadcast(f32[1024,32]{1,0:T(8,128)S(1)} %bitcast.63), dimensions={0,1} | broadcast | bytes 8519680 | tf_op jit(solution)/shard_map/jit(clip)/min | solution.py:86
  97.3 0.0 slice-done
  97.3 0.0 slice-done.1
  97.3 6.5 %fusion.1 = bf16[1024,4096]{1,0:T(8,128)(2,1)} fusion(bf16[1024,4096]{1,0:T(8,128)(2,1)S(1)} %bitcast.58, bf16[128,8,32,128]{3,2,1,0:T(8,128)(2,1)S(1)} %bitcast.59, bf16[128,8,32,128]{3,2,1,0:T(8,128)(2,1)S(1)} %bitcast.60), kind=kLoop, calls=%fused_computation.3 | loop fusion | flops 8388608 | bytes 33554432 | tf_op jit(solution)/shard_map/convert_element_type | solution.py:136
  103.8 13.1 %convert_element_type.63 = bf16[32,8,4,4096]{3,2,1,0:T(4,128)(2,1)} reshape(bf16[1024,4096]{1,0:T(8,128)(2,1)} %fusion.1) | data formatting | bytes 16777216 | tf_op jit(solution)/shard_map/convert_element_type | solution.py:21
  117.0 15.5 %copy.42 = bf16[32,8,4,4096]{3,1,2,0:T(8,128)(2,1)} copy(bf16[32,8,4,4096]{3,2,1,0:T(4,128)(2,1)} %convert_element_type.63) | data formatting | bytes 16777216 | tf_op jit(solution)/shard_map/convert_element_type | solution.py:21
  132.5 0.0 reduce-scatter.3.cloned.1.call-update
  132.5 0.3 reduce-scatter.5.cloned.1.call-start
  132.7 98.6 %reduce-scatter.3.cloned.1.call-done = bf16[4,8,4,4096]{3,1,2,0:T(8,128)(2,1)} async-done(((bf16[32,8,4,4096]{3,1,2,0:T(8,128)(2,1)}), bf16[4,8,4,4096]{3,1,2,0:T(8,128)(2,1)}) %reduce-scatter.3.cloned.1.call-update) | async-done | bytes 1048592 | tf_op jit(solution)/shard_map/reduce_scatter | solution.py:23
  231.4 0.0 reduce-scatter.5.cloned.1.call-update
  231.4 25.8 %reduce-scatter.5.cloned.1.call-done = bf16[1,8,4,4096]{3,1,2,0:T(8,128)(2,1)} async-done(((bf16[4,8,4,4096]{3,1,2,0:T(8,128)(2,1)}), bf16[1,8,4,4096]{3,1,2,0:T(8,128)(2,1)}) %reduce-scatter.5.cloned.1.call-update) | async-done | bytes 262160 | tf_op jit(solution)/shard_map/reduce_scatter | solution.py:23
  257.3 1.9 copy.43
  259.1 6.3 %all-to-all-start = ((bf16[8,1,1,4,4096]{4,3,2,1,0:T(4,128)(2,1)}), bf16[8,1,1,4,4096]{4,3,2,1,0:T(4,128)(2,1)S(1)}, u32[]{:S(2)}, u32[]{:S(2)}) async-start(bf16[8,1,1,4,4096]{4,3,2,1,0:T(4,128)(2,1)} %copy.43), calls=%async_computation.2 | async-start | bytes 524288 | tf_op jit(solution)/shard_map/all_to_all | solution.py:34
  265.4 0.1 broadcast_bitcast_fusion
  265.5 6.4 %all-to-all-done = bf16[8,1,1,4,4096]{4,3,2,1,0:T(4,128)(2,1)S(1)} async-done(((bf16[8,1,1,4,4096]{4,3,2,1,0:T(4,128)(2,1)}), bf16[8,1,1,4,4096]{4,3,2,1,0:T(4,128)(2,1)S(1)}, u32[]{:S(2)}, u32[]{:S(2)}) %all-to-all-start) | async-done | bytes 262176 | tf_op jit(solution)/shard_map/all_to_all | solution.py:34
  271.9 0.1 convert_reduce_fusion
  272.0 0.1 reshape_reshape.4
  272.1 0.3 convolution_multiply_fusion.2
  272.4 0.0 copy-done.1
  272.4 0.0 copy-done.2
  272.4 0.0 copy-done.3
  272.4 1.7 fusion.22
  274.1 0.1 broadcast_in_dim.2
  274.2 9.9 %all_to_all.10 = bf16[8,1,1,4,4096]{4,3,2,1,0:T(4,128)(2,1)S(1)} all-to-all(bf16[8,1,1,4,4096]{4,3,2,1,0:T(4,128)(2,1)S(1)} %broadcast_in_dim.2), channel_id=1, replica_groups=mesh['outer'=8,'inner_0'=8,'inner_1'=4] {'outer'}, dimensions={0} | all-to-all | bytes 524288 | tf_op jit(solution)/shard_map/all_to_all | solution.py:40
  284.1 0.9 copy.44
  285.0 0.0 all-gather.3.cloned.1.call-update
  285.0 15.5 %reshape.78 = f32[8,32,4,4096]{3,2,1,0:T(4,128)} reshape(bf16[1024,4096]{1,0:T(8,128)(2,1)} %param.12) | data formatting | bytes 25165824 | tf_op jit(solution)/shard_map/convert_element_type | solution.py:153
  300.5 80.9 %all-gather.3.cloned.1.call-done = bf16[8,32,1,4,4096]{4,0,3,2,1:T(8,128)(2,1)} async-done(((bf16[8,1,1,4,4096]{4,0,3,2,1:T(8,128)(2,1)}), bf16[8,32,1,4,4096]{4,0,3,2,1:T(8,128)(2,1)}) %all-gather.3.cloned.1.call-update) | async-done | bytes 8388624 | tf_op jit(solution)/shard_map/all_gather | solution.py:154
  381.4 13.8 %fusion.2 = bf16[8,32,4,4096]{3,2,1,0:T(4,128)(2,1)S(1)} fusion(f32[8,32,4,4096]{3,2,1,0:T(4,128)} %reshape.78, bf16[8,32,1,4,4096]{4,0,3,2,1:T(8,128)(2,1)} %all-gather.3.cloned.1.call-done), kind=kLoop, calls=%fused_computation.5 | loop fusion | flops 12582912 | bytes 33554432 | tf_op jit(solution)/shard_map/convert_element_type | solution.py:155
  395.2 5.0 %fusion.11 = bf16[384,8,32,4]{0,1,3,2:T(8,128)(2,1)S(1)} fusion(bf16[384,4096]{1,0:T(8,128)(2,1)S(1)} %copy-done, bf16[8,32,4,4096]{3,2,1,0:T(4,128)(2,1)S(1)} %fusion.2), kind=kOutput, calls=%fused_computation.11 | convolution fusion | flops 3221618688 | bytes 12320768 | tf_op jit(solution)/shard_map/dot_general | solution.py:156
  400.2 0.3 copy.47
  400.5 0.2 convert_element_type.71
  400.7 1.2 copy.48
  (15 shorter events, 0.1 us)
Async XLA Ops:
  7.2 224.2 %reduce-scatter.3.cloned.1.call-start = ((), (), s32[]{:S(2)}) async-start(), calls=%async_computation.4 | async-start | bytes 9437184 | tf_op jit(solution)/shard_map/reduce_scatter | solution.py:23
  61.8 13.4 %copy-start.4 = (s32[1,8,32]{2,1,0:T(8,128)S(1)}, s32[1,8,32]{2,1,0:T(8,128)}, u32[]{:S(2)}) copy-start(s32[1,8,32]{2,1,0:T(8,128)} %param.15) | copy-start | bytes 3076
  75.3 22.0 %slice-start = ((s8[8388608]{0:T(1024)(128)(4,1)}), s8[4194304]{0:T(1024)(128)(4,1)S(1)}, s32[]{:S(2)}) async-start(s8[8388608]{0:T(1024)(128)(4,1)} %bitcast.57), calls=%async_computation.7 | async-start | bytes 8388608
  87.1 10.3 %slice-start.1 = ((s8[8388608]{0:T(1024)(128)(4,1)}), s8[4194304]{0:T(1024)(128)(4,1)S(1)}, s32[]{:S(2)}) async-start(s8[8388608]{0:T(1024)(128)(4,1)} %bitcast.57), calls=%async_computation.8 | async-start | bytes 8388608
  132.4 133.0 %copy-start.5 = (s32[4,32]{1,0:T(4,128)S(1)}, s32[4,32]{1,0:T(4,128)}, u32[]{:S(2)}) copy-start(s32[4,32]{1,0:T(4,128)} %param.16) | copy-start | bytes 1540
  132.4 140.0 %copy-start.1 = (f32[4,4096]{1,0:T(4,128)S(1)}, f32[4,4096]{1,0:T(4,128)}, u32[]{:S(2)}) copy-start(f32[4,4096]{1,0:T(4,128)} %param.11) | copy-start | bytes 196612
  132.4 140.0 %copy-start.2 = (f32[4,4096]{1,0:T(4,128)S(1)}, f32[4,4096]{1,0:T(4,128)}, u32[]{:S(2)}) copy-start(f32[4,4096]{1,0:T(4,128)} %param.13) | copy-start | bytes 196612
  132.4 140.0 %copy-start.3 = (f32[4,4096]{1,0:T(4,128)S(1)}, f32[4,4096]{1,0:T(4,128)}, u32[]{:S(2)}) copy-start(f32[4,4096]{1,0:T(4,128)} %param.14) | copy-start | bytes 196612
  132.5 124.8 %reduce-scatter.5.cloned.1.call-start = ((), (), s32[]{:S(2)}) async-start(), calls=%async_computation.5 | async-start | bytes 1310720 | tf_op jit(solution)/shard_map/reduce_scatter | solution.py:23
  259.1 12.8 %all-to-all-start = ((bf16[8,1,1,4,4096]{4,3,2,1,0:T(4,128)(2,1)}), bf16[8,1,1,4,4096]{4,3,2,1,0:T(4,128)(2,1)S(1)}, u32[]{:S(2)}, u32[]{:S(2)}) async-start(bf16[8,1,1,4,4096]{4,3,2,1,0:T(4,128)(2,1)} %copy.43), calls=%async_computation.2 | async-start | bytes 524288 | tf_op jit(solution)/shard_map/all_to_all | solution.py:34
  265.4 115.9 %all-gather.3.cloned.1.call-start = ((), (), s32[]{:S(2)}) async-start(), calls=%async_computation.6 | async-start | bytes 8650752 | tf_op jit(solution)/shard_map/all_gather | solution.py:154
  300.5 94.7 %copy-start = (bf16[384,4096]{1,0:T(8,128)(2,1)S(1)}, bf16[384,4096]{1,0:T(8,128)(2,1)}, u32[]{:S(2)}) copy-start(bf16[384,4096]{1,0:T(8,128)(2,1)} %param.9) | copy-start | bytes 9437188
Sparse Core Ops, SparseCore 0:
  132.6 98.7 reduce-scatter.2
  233.9 23.2 reduce-scatter.4
  285.1 96.2 all-gather.2
where the time goes:
time: 410 us; the launch traced here: 408 us
  waiting for transfers between devices  212 us (52%)
  local copies, waits for them, and re-layouts  117 us (29%)
  matrix products  26.3 us (6%)
  other arithmetic  22.9 us (6%)
  between operations  13.9 us (3%)
  blocking collectives  9.94 us (2%)
  starting transfers between devices  6.6 us (2%)
    reduce_scatter x2, waiting for transfers between devices, summed_rows(): running = lax.psum_scatter(running, axis, scatter_dimension=0, tiled=True)  124 us
    all_gather x1, waiting for transfers between devices, shards(): lax.all_gather(outer_part, INNER, axis=1, tiled=True).astype(jnp.float32)  80.9 us
    convert_element_type x2, local copies, waits for them, and re-layouts, summed_rows(): running = terms.astype(jnp.bfloat16)  28.6 us
    mul x1, local copies, waits for them, and re-layouts, rotate_rows(): row_block.reshape(row_count, sign_rows.shape[0], sign_rows.shape[1])  20.2 us
    convert_element_type x1, local copies, waits for them, and re-layouts, shards(): base_grid.astype(jnp.float32)  15.5 us
    dot_general x1, matrix products, rotate_rows(): jnp.dot(blocks.reshape(-1, sign_rows.shape[1]), matrix, precision=highest)  15.3 us
    convert_element_type x1, other arithmetic, shards(): effective = (base_grid.astype(jnp.float32) + lax.all_gather(outer_part, I...  13.8 us
    div x1, local copies, waits for them, and re-layouts, rotate_rows(): return turned.reshape(row_block.shape) / math.sqrt(sign_rows.shape[1])  13.4 us
  transfers between devices with their start and end apart: 4, of which 4 were waited for; matrix products, arithmetic and copies ran while one was open for 4% of the time, Pallas kernels for 0%

commit v1 on v0

--- a/solution.py
+++ b/solution.py
@@ -15,6 +15,12 @@
 decay_rate = 0.1
 adam_eps = 1e-08
 highest = lax.Precision.HIGHEST
+_put_stacks_all = lambda x0, ax_name: jnp.concatenate(
+    jax.lax.all_to_all(
+        jnp.stack([x0 for _ in range(jax.lax.axis_size(ax_name))], axis=0), ax_name, 0, 0
+    ),
+    1,
+)
 
 
 def summed_rows(terms, axes):
@@ -150,8 +156,7 @@
     outer_part = gathered_copies(diff_coded.reshape(1, 1, rows_dev, model_width), "outer", 0)
     base_grid = base_weights.reshape(outer_count, inner_count, rows_dev, model_width)
     effective = (
-        base_grid.astype(jnp.float32)
-        + lax.all_gather(outer_part, INNER, axis=1, tiled=True).astype(jnp.float32)
+        base_grid.astype(jnp.float32) + _put_stacks_all(outer_part, INNER).astype(jnp.float32)
     ).astype(jnp.bfloat16)
     result = lax.dot_general(
         tokens, effective, (((1,), (3,)), ((), ())), preferred_element_type=jnp.float32

time: 410 us -> 546 us (1.33)
  the two profiles are of different devices: /device:TPU:1 before, /device:TPU:118 now
where the time goes in v1:
time: 546 us; the launch traced here: 536 us
  waiting for transfers between devices  307 us (56%)
  local copies, waits for them, and re-layouts  136 us (25%)
  matrix products  44.1 us (8%)
  starting transfers between devices  15.2 us (3%)
  between operations  14.7 us (3%)
  blocking collectives  9.93 us (2%)
  other arithmetic  9.01 us (2%)
    all_to_all x1, waiting for transfers between devices, jax.lax.all_to_all(jnp.stack([x0 for _ in range(jax.lax.axis_size(ax_name...  180 us
    reduce_scatter x2, waiting for transfers between devices, summed_rows(): running = lax.psum_scatter(running, axis, scatter_dimension=0, tiled=True)  122 us
    convert_element_type x2, local copies, waits for them, and re-layouts, summed_rows(): running = terms.astype(jnp.bfloat16)  28.6 us
    dot_general x1, matrix products, shards(): lax.dot_general(tokens, effective, (((1,), (3,)), ((), ())), preferred_el...  22.8 us
    min x1, local copies, waits for them, and re-layouts, clip_rows(): return jnp.clip(shaped, -limits, limits).reshape(row_block.shape)  21.5 us
    mul x1, local copies, waits for them, and re-layouts, rotate_rows(): row_block.reshape(row_count, sign_rows.shape[0], sign_rows.shape[1])  20.2 us
    convert_element_type x1, local copies, waits for them, and re-layouts, shards(): base_grid.astype(jnp.float32)  15.6 us
    dot_general x1, matrix products, rotate_rows(): jnp.dot(blocks.reshape(-1, sign_rows.shape[1]), matrix, precision=highest)  15.3 us
  transfers between devices with their start and end apart: 4, of which 4 were waited for; matrix products, arithmetic and copies ran while one was open for 3% of the time, Pallas kernels for 0%

profile of v1, /device:TPU:118, one launch (start us, length us, event | category | flops | bytes accessed | tf_op | source)
XLA Modules:
  0.0 536.0 jit_solution(16071557389293420566)
XLA Ops:
  7.2 0.0 reduce-scatter.3.cloned.1.call-start
  7.2 0.7 fusion.32
  7.9 3.4 copy.61
  11.4 2.3 copy.47
  13.7 2.4 reshape.78
  16.0 2.3 copy.48
  18.3 2.3 reshape.84
  20.6 5.7 %convolution_multiply_fusion.1 = f32[1024,32,128]{2,0,1:T(8,128)S(1)} fusion(bf16[384,1024,1]{0,1,2:T(8,128)(2,1)} %reshape.84, bf16[32,128,384]{2,1,0:T(8,128)(2,1)S(1)} %bitcast.63, f32[32,128]{1,0:T(8,128)S(1)} %get-tuple-element.29), kind=kOutput, calls=%fused_computation.6 | convolution fusion | flops 3225419776 | bytes 20725760 | tf_op jit(solution)/shard_map/dot_general | solution.py:135
  26.3 20.2 %copy.50 = f32[1024,32,128]{2,1,0:T(8,128)S(1)} copy(f32[1024,32,128]{2,0,1:T(8,128)S(1)} %convolution_multiply_fusion.1) | data formatting | bytes 33554432 | tf_op jit(solution)/shard_map/mul | solution.py:73
  46.5 15.3 %convolution_multiply_fusion = bf16[32768,128]{1,0:T(8,128)(2,1)} fusion(f32[32768,128]{1,0:T(8,128)S(1)} %bitcast.58), kind=kOutput, calls=%fused_computation | convolution fusion | flops 6451412992 | bytes 25165824 | tf_op jit(solution)/shard_map/dot_general | solution.py:74
  61.8 13.3 %div.31 = bf16[1024,4096]{1,0:T(8,128)(2,1)} reshape(bf16[32768,128]{1,0:T(8,128)(2,1)} %convolution_multiply_fusion) | data formatting | bytes 16777216 | tf_op jit(solution)/shard_map/div | solution.py:75
  75.1 0.0 copy-done.4
  75.1 0.1 transpose.23
  75.3 0.0 slice-start
  75.3 11.7 %max.32 = bf16[1024,32,128]{2,1,0:T(8,128)(2,1)S(1)} broadcast(bf16[1024,32]{1,0:T(8,128)(2,1)S(1)} %neg.13), dimensions={0,1} | broadcast | bytes 8454144 | tf_op jit(solution)/shard_map/jit(clip)/max | solution.py:92
  87.0 0.0 slice-start.1
  87.1 21.5 %min.35 = bf16[1024,32,128]{2,1,0:T(8,128)(2,1)S(1)} broadcast(f32[1024,32]{1,0:T(8,128)S(1)} %bitcast.65), dimensions={0,1} | broadcast | bytes 8519680 | tf_op jit(solution)/shard_map/jit(clip)/min | solution.py:92
  108.5 0.0 slice-done
  108.6 0.0 slice-done.1
  108.6 6.5 %fusion.1 = bf16[1024,4096]{1,0:T(8,128)(2,1)} fusion(bf16[1024,4096]{1,0:T(8,128)(2,1)S(1)} %bitcast.60, bf16[128,8,32,128]{3,2,1,0:T(8,128)(2,1)S(1)} %bitcast.61, bf16[128,8,32,128]{3,2,1,0:T(8,128)(2,1)S(1)} %bitcast.62), kind=kLoop, calls=%fused_computation.3 | loop fusion | flops 8388608 | bytes 33554432 | tf_op jit(solution)/shard_map/convert_element_type | solution.py:142
  115.0 13.1 %convert_element_type.69 = bf16[32,8,4,4096]{3,2,1,0:T(4,128)(2,1)} reshape(bf16[1024,4096]{1,0:T(8,128)(2,1)} %fusion.1) | data formatting | bytes 16777216 | tf_op jit(solution)/shard_map/convert_element_type | solution.py:27
  128.2 15.5 %copy.51 = bf16[32,8,4,4096]{3,1,2,0:T(8,128)(2,1)} copy(bf16[32,8,4,4096]{3,2,1,0:T(4,128)(2,1)} %convert_element_type.69) | data formatting | bytes 16777216 | tf_op jit(solution)/shard_map/convert_element_type | solution.py:27
  143.7 0.0 reduce-scatter.3.cloned.1.call-update
  143.7 0.0 reduce-scatter.5.cloned.1.call-start
  143.7 96.1 %reduce-scatter.3.cloned.1.call-done = bf16[4,8,4,4096]{3,1,2,0:T(8,128)(2,1)} async-done(((bf16[32,8,4,4096]{3,1,2,0:T(8,128)(2,1)}), bf16[4,8,4,4096]{3,1,2,0:T(8,128)(2,1)}) %reduce-scatter.3.cloned.1.call-update) | async-done | bytes 1048592 | tf_op jit(solution)/shard_map/reduce_scatter | solution.py:29
  239.8 0.0 reduce-scatter.5.cloned.1.call-update
  239.8 25.9 %reduce-scatter.5.cloned.1.call-done = bf16[1,8,4,4096]{3,1,2,0:T(8,128)(2,1)} async-done(((bf16[4,8,4,4096]{3,1,2,0:T(8,128)(2,1)}), bf16[1,8,4,4096]{3,1,2,0:T(8,128)(2,1)}) %reduce-scatter.5.cloned.1.call-update) | async-done | bytes 262160 | tf_op jit(solution)/shard_map/reduce_scatter | solution.py:29
  265.7 1.9 copy.52
  267.6 4.8 all-to-all-start
  272.4 0.0 copy-done.5
  272.4 0.1 broadcast_bitcast_fusion
  272.5 4.3 all-to-all-done
  276.8 0.1 convert_reduce_fusion
  276.9 0.1 reshape_reshape.4
  276.9 0.3 convolution_multiply_fusion.2
  277.3 1.7 fusion.14
  279.0 0.1 broadcast_in_dim.2
  279.0 9.9 %all_to_all.15 = bf16[8,1,1,4,4096]{4,3,2,1,0:T(4,128)(2,1)S(1)} all-to-all(bf16[8,1,1,4,4096]{4,3,2,1,0:T(4,128)(2,1)S(1)} %broadcast_in_dim.2), channel_id=1, replica_groups=mesh['outer'=8,'inner_0'=8,'inner_1'=4] {'outer'}, dimensions={0} | all-to-all | bytes 524288 | tf_op jit(solution)/shard_map/all_to_all | solution.py:46
  289.0 7.5 %stack.3 = bf16[32,8,1,4,4096]{4,3,1,2,0:T(4,128)(2,1)} broadcast(bf16[8,4,4096]{2,1,0:T(4,128)(2,1)S(1)} %bitcast.69), dimensions={1,3,4} | broadcast | bytes 8650752 | tf_op jit(solution)/shard_map/stack | solution.py:20
  296.4 10.3 %all-to-all-start.2 = ((bf16[32,8,1,4,4096]{4,3,1,2,0:T(4,128)(2,1)}), bf16[32,8,1,4,4096]{4,3,1,2,0:T(4,128)(2,1)}, u32[]{:S(2)}, u32[]{:S(2)}) async-start(bf16[32,8,1,4,4096]{4,3,1,2,0:T(4,128)(2,1)} %stack.3), calls=%async_computation.4 | async-start | bytes 16777216 | tf_op jit(solution)/shard_map/all_to_all | solution.py:19
  306.7 0.0 copy-start
  306.7 15.6 %reshape.82 = f32[8,32,4,4096]{3,2,1,0:T(4,128)} reshape(bf16[1024,4096]{1,0:T(8,128)(2,1)} %param.12) | data formatting | bytes 25165824 | tf_op jit(solution)/shard_map/convert_element_type | solution.py:159
  322.3 180.4 %all-to-all-done.2 = bf16[32,8,1,4,4096]{4,3,1,2,0:T(4,128)(2,1)} async-done(((bf16[32,8,1,4,4096]{4,3,1,2,0:T(4,128)(2,1)}), bf16[32,8,1,4,4096]{4,3,1,2,0:T(4,128)(2,1)}, u32[]{:S(2)}, u32[]{:S(2)}) %all-to-all-start.2) | async-done | bytes 8388640 | tf_op jit(solution)/shard_map/all_to_all | solution.py:19
  502.7 22.8 %fusion.3 = bf16[8,32,4,384]{3,0,2,1:T(8,128)(2,1)} fusion(f32[8,32,4,4096]{3,2,1,0:T(4,128)} %reshape.82, bf16[32,8,1,4,4096]{4,3,1,2,0:T(4,128)(2,1)} %all-to-all-done.2, bf16[384,4096]{1,0:T(8,128)(2,1)S(1)} %copy-done), kind=kOutput, calls=%fused_computation.7 | convolution fusion | flops 3233808384 | bytes 29097984 | tf_op jit(solution)/shard_map/dot_general | solution.py:161
  525.6 1.4 copy.79
  527.0 0.4 copy.56
  527.4 0.2 convert_element_type.79
  527.6 1.2 copy.57
  (14 shorter events, 0.1 us)
Async XLA Ops:
  7.2 232.7 %reduce-scatter.3.cloned.1.call-start = ((), (), s32[]{:S(2)}) async-start(), calls=%async_computation.5 | async-start | bytes 9437184 | tf_op jit(solution)/shard_map/reduce_scatter | solution.py:29
  61.8 13.3 %copy-start.4 = (s32[1,8,32]{2,1,0:T(8,128)S(1)}, s32[1,8,32]{2,1,0:T(8,128)}, u32[]{:S(2)}) copy-start(s32[1,8,32]{2,1,0:T(8,128)} %param.15) | copy-start | bytes 3076
  75.3 33.3 %slice-start = ((s8[8388608]{0:T(1024)(128)(4,1)}), s8[4194304]{0:T(1024)(128)(4,1)S(1)}, s32[]{:S(2)}) async-start(s8[8388608]{0:T(1024)(128)(4,1)} %bitcast.59), calls=%async_computation.7 | async-start | bytes 8388608
  87.0 21.5 %slice-start.1 = ((s8[8388608]{0:T(1024)(128)(4,1)}), s8[4194304]{0:T(1024)(128)(4,1)S(1)}, s32[]{:S(2)}) async-start(s8[8388608]{0:T(1024)(128)(4,1)} %bitcast.59), calls=%async_computation.8 | async-start | bytes 8388608
  143.6 128.8 %copy-start.5 = (s32[4,32]{1,0:T(4,128)S(1)}, s32[4,32]{1,0:T(4,128)}, u32[]{:S(2)}) copy-start(s32[4,32]{1,0:T(4,128)} %param.16) | copy-start | bytes 1540
  143.6 133.6 %copy-start.1 = (f32[4,4096]{1,0:T(4,128)S(1)}, f32[4,4096]{1,0:T(4,128)}, u32[]{:S(2)}) copy-start(f32[4,4096]{1,0:T(4,128)} %param.11) | copy-start | bytes 196612
  143.6 133.6 %copy-start.2 = (f32[4,4096]{1,0:T(4,128)S(1)}, f32[4,4096]{1,0:T(4,128)}, u32[]{:S(2)}) copy-start(f32[4,4096]{1,0:T(4,128)} %param.13) | copy-start | bytes 196612
  143.6 133.6 %copy-start.3 = (f32[4,4096]{1,0:T(4,128)S(1)}, f32[4,4096]{1,0:T(4,128)}, u32[]{:S(2)}) copy-start(f32[4,4096]{1,0:T(4,128)} %param.14) | copy-start | bytes 196612
  143.7 122.1 %reduce-scatter.5.cloned.1.call-start = ((), (), s32[]{:S(2)}) async-start(), calls=%async_computation.6 | async-start | bytes 1310720 | tf_op jit(solution)/shard_map/reduce_scatter | solution.py:29
  267.6 9.2 %all-to-all-start = ((bf16[8,1,1,4,4096]{4,3,2,1,0:T(4,128)(2,1)}), bf16[8,1,1,4,4096]{4,3,2,1,0:T(4,128)(2,1)S(1)}, u32[]{:S(2)}, u32[]{:S(2)}) async-start(bf16[8,1,1,4,4096]{4,3,2,1,0:T(4,128)(2,1)} %copy.52), calls=%async_computation.2 | async-start | bytes 524288 | tf_op jit(solution)/shard_map/all_to_all | solution.py:40
  296.4 206.3 %all-to-all-start.2 = ((bf16[32,8,1,4,4096]{4,3,1,2,0:T(4,128)(2,1)}), bf16[32,8,1,4,4096]{4,3,1,2,0:T(4,128)(2,1)}, u32[]{:S(2)}, u32[]{:S(2)}) async-start(bf16[32,8,1,4,4096]{4,3,1,2,0:T(4,128)(2,1)} %stack.3), calls=%async_computation.4 | async-start | bytes 16777216 | tf_op jit(solution)/shard_map/all_to_all | solution.py:19
  306.7 196.0 %copy-start = (bf16[384,4096]{1,0:T(8,128)(2,1)S(1)}, bf16[384,4096]{1,0:T(8,128)(2,1)}, u32[]{:S(2)}) copy-start(bf16[384,4096]{1,0:T(8,128)(2,1)} %param.9) | copy-start | bytes 9437188
Sparse Core Ops, SparseCore 0:
  143.8 95.9 reduce-scatter.2
  242.4 23.3 reduce-scatter.4
